TPU v7x, 32 devices: a whole 2x2x4 slice. The times are simulated.
32 devices in a mesh: chan: 16 (over z, y, core), band: 2 (over x).
Axes of the slice: x: 2, y: 2, z: 4, core: 2. Of those that a mesh axis runs over, the one named last changes fastest.
Arguments:
- strain: bfloat16 [4096, 4, 4096], P('chan', None, 'band'), may hold values from -6 to 6
- band_start: int32 [2], replicated, may hold values from 4 to 818
Outputs:
- coherency: bfloat16 [2, 2, 4096, 4096], P('band', None, 'chan')
All inputs are finite; a program needn't handle non-finite values.
Results may differ from a plain program's by a relative error of at most 0.0056.
Values may be sent and summed in bfloat16 or wider, within the bound.
A program may use at most 64 MiB of HBM per device.

v0:
```python
import math

import jax
import jax.numpy as jnp
from jax import lax
from jax.sharding import PartitionSpec as P

WINDOW_SAMPLES = 4096
K = 32


def dft_table(freqs, positions):
    phase_angles = positions[:, None, None] * freqs[None, :, :] % WINDOW_SAMPLES
    angles = phase_angles.astype(jnp.float32) * (2.0 * math.pi / WINDOW_SAMPLES)
    taper = 0.5 - 0.5 * jnp.cos(positions.astype(jnp.float32) * (2.0 * math.pi / WINDOW_SAMPLES))
    cosine = taper[:, None, None] * jnp.cos(angles)
    sine = -taper[:, None, None] * jnp.sin(angles)
    return jnp.concatenate([cosine, sine], axis=2).astype(jnp.bfloat16)


def whiten(spectrum, chans, windows):
    power = jnp.mean(spectrum * spectrum, axis=1, keepdims=True)
    whitened = (spectrum * lax.rsqrt(power + 1e-06)).astype(jnp.bfloat16)
    return (
        whitened.reshape(chans, windows, 2, K).transpose(0, 2, 1, 3).reshape(chans, 2 * windows * K)
    )


def cross_block(local_panel_rows, other_panel):
    half_feat = other_panel.shape[1] // 2
    rotated = jnp.concatenate([-other_panel[:, half_feat:], other_panel[:, :half_feat]], axis=1)
    stacked_spectra = jnp.stack([other_panel, rotated])
    cross_product = jnp.einsum(
        "gb,ozb->ogz", local_panel_rows, stacked_spectra, preferred_element_type=jnp.float32
    )
    return (cross_product * (1.0 / (2.0 * K))).astype(jnp.bfloat16)


def shards(strain, band_start):
    chans, windows, samp_dev = strain.shape
    flat = strain.reshape(chans * windows, samp_dev)
    band_index = lax.axis_index("band")
    bins = jnp.arange(K, dtype=jnp.int32)
    positions = band_index * samp_dev + jnp.arange(samp_dev, dtype=jnp.int32)
    own_rows = band_start.shape[0] // lax.axis_size("band")
    table = dft_table(band_start[:, None] + bins[None, :], positions)
    partial_sum = jnp.dot(
        flat,
        table.reshape(samp_dev, own_rows * lax.axis_size("band") * 2 * K),
        preferred_element_type=jnp.float32,
    )
    spectrum = lax.psum_scatter(
        partial_sum.reshape(chans * windows, own_rows * lax.axis_size("band"), 2 * K).transpose(
            1, 0, 2
        ),
        "band",
        scatter_dimension=0,
        tiled=True,
    )[0]
    panel = whiten(spectrum, chans, windows)
    result = cross_block(panel, lax.all_gather(panel, "chan", axis=0, tiled=True))
    return result[None]


def solution(mesh):
    return jax.shard_map(
        shards,
        mesh=mesh,
        in_specs=(P("chan", None, "band"), P()),
        out_specs=P("band", None, "chan", None),
        check_vma=False,
    )
```

profile of v0, /device:TPU:0, one launch (start us, length us, event | category | flops | bytes accessed | tf_op | source)
XLA Modules:
  0.0 110.6 jit_solution(17581041792112892675)
XLA Ops:
  6.5 0.0 reduce-scatter.2.cloned.1.call-start
  6.5 0.1 multiply_subtract_fusion
  6.6 0.7 iota_add_fusion.1
  7.3 6.9 %reshape.73 = bf16[1024,2048]{1,0:T(8,128)(2,1)} reshape(bf16[256,4,2048]{2,1,0:T(4,128)(2,1)} %param.2) | data formatting | bytes 8388608 | tf_op jit(solution)/shard_map/reshape | solution.py:41
  14.2 2.3 %multiply_convert_fusion.3 = (bf16[2048,2,32]{0,2,1:T(8,128)(2,1)S(1)}, bf16[2048,2,32]{0,2,1:T(8,128)(2,1)S(1)}) fusion(s32[2,32]{1,0:T(2,128)S(1)} %iota_add_fusion.1, s32[2048]{0:T(1024)S(1)} %iota_add_fusion, f32[2048]{0:T(1024)S(1)} %get-tuple-element.9, f32[2048]{0:T(1024)S(1)} %get-tuple-element.10), kind=kLoop, calls=%fused_computation.20 | loop fusion | flops 2359296 | bytes 549120 | tf_op jit(solution)/shard_map/convert
  16.5 3.7 %fusion.10 = f32[128,1024]{1,0:T(8,128)S(1)} fusion(bf16[2048,128]{0,1:T(8,128)(2,1)S(1)} %bitcast.22, bf16[1024,2048]{1,0:T(8,128)(2,1)} %reshape.73), kind=kOutput, calls=%fused_computation.27 | convolution fusion | flops 536870912 | bytes 5242880 | tf_op jit(solution)/shard_map/dot_general | solution.py:47
  20.2 1.3 %copy.5 = f32[1024,2,64]{2,0,1:T(8,128)} copy(f32[1024,2,64]{0,2,1:T(8,128)S(1)} %bitcast.21) | data formatting | bytes 1048576 | tf_op jit(solution)/shard_map/reshape | solution.py:53
  21.5 0.0 reduce-scatter.2.cloned.1.call-update
  21.6 0.0 all-gather.2.cloned.1.call-start
  21.6 23.2 %reduce-scatter.2.cloned.1.call-done = f32[1,1024,64]{2,1,0:T(8,128)} async-done(((f32[2,1024,64]{2,1,0:T(8,128)}), f32[1,1024,64]{2,1,0:T(8,128)}) %reduce-scatter.2.cloned.1.call-update) | async-done | bytes 262160 | tf_op jit(solution)/shard_map/reduce_scatter | solution.py:52
  44.8 1.2 %multiply_reduce_fusion = f32[1024]{0:T(1024)S(1)} fusion(f32[1,1024,64]{2,1,0:T(8,128)} %reduce-scatter.2.cloned.1.call-done), kind=kLoop, calls=%fused_computation.18 | loop fusion | flops 130048 | bytes 266240 | tf_op jit(solution)/shard_map/reduce_sum | solution.py:22
  46.1 0.1 rsqrt.12
  46.2 1.7 %squeeze.3 = f32[256,4,2,32]{3,2,1,0:T(2,128)S(1)} reshape(f32[1,1024,64]{2,1,0:T(8,128)} %reduce-scatter.2.cloned.1.call-done) | data formatting | bytes 524288 | tf_op jit(solution)/shard_map/squeeze | solution.py:52
  47.9 1.7 %fusion.7 = bf16[256,2,4,32]{3,1,2,0:T(2,128)(2,1)S(1)} fusion(f32[256,4,2,32]{3,2,1,0:T(2,128)S(1)} %squeeze.3, f32[256,4]{1,0:T(8,128)S(1)} %rsqrt.12), kind=kLoop, calls=%fused_computation.16 | loop fusion | flops 131072 | bytes 397312 | tf_op jit(solution)/shard_map/transpose | solution.py:25
  49.6 0.5 copy.6
  50.1 0.8 copy.7
  50.8 0.0 all-gather.2.cloned.1.call-update
  50.9 41.6 %all-gather.2.cloned.1.call-done = bf16[4096,256]{1,0:T(8,128)(2,1)} async-done(((bf16[256,256]{1,0:T(8,128)(2,1)}), bf16[4096,256]{1,0:T(8,128)(2,1)}) %all-gather.2.cloned.1.call-update) | async-done | bytes 2097168 | tf_op jit(solution)/shard_map/all_gather | solution.py:61
  92.5 0.0 copy-start
  92.5 1.9 %slice_negate_fusion = (bf16[4096,128]{1,0:T(8,128)(2,1)S(1)}, bf16[4096,128]{1,0:T(8,128)(2,1)S(1)}) fusion(bf16[4096,256]{1,0:T(8,128)(2,1)} %all-gather.2.cloned.1.call-done), kind=kLoop, calls=%fused_computation.6 | loop fusion | flops 524288 | bytes 4194304 | tf_op jit(solution)/shard_map/neg | solution.py:31
  94.4 0.2 maximum_bitcast_fusion
  94.6 0.1 copy-done
  94.7 2.7 %fusion = bf16[1,2,256,4096]{2,3,1,0:T(8,128)(2,1)} fusion(bf16[256,256,1]{0,1,2:T(8,128)(2,1)S(1)} %bitcast.25, bf16[1,4096,256]{2,1,0:T(8,128)(2,1)S(1)} %maximum_bitcast_fusion, bf16[1,4096,256]{2,1,0:T(8,128)(2,1)S(1)} %bitcast.23), kind=kOutput, calls=%fused_computation.1 | convolution fusion | flops 1080033280 | bytes 8519680 | tf_op jit(solution)/shard_map/gb,ozb->ogz/dot_general | solution.py:33
  97.4 6.3 %copy.9 = bf16[1,2,256,4096]{3,2,1,0:T(8,128)(2,1)} copy(bf16[1,2,256,4096]{2,3,1,0:T(8,128)(2,1)} %fusion) | data formatting | bytes 8388608 | tf_op jit(solution)/shard_map/broadcast_in_dim | solution.py:62
  (3 shorter events, 0.0 us)
Async XLA Ops:
  6.5 38.3 %reduce-scatter.2.cloned.1.call-start = ((), (), s32[]{:S(2)}) async-start(), calls=%async_computation.1 | async-start | bytes 1572864 | tf_op jit(solution)/shard_map/reduce_scatter | solution.py:52
  21.6 70.9 %all-gather.2.cloned.1.call-start = ((), (), s32[]{:S(2)}) async-start(), calls=%async_computation.2 | async-start | bytes 2228224 | tf_op jit(solution)/shard_map/all_gather | solution.py:61
  92.5 2.2 %copy-start = (bf16[4096,256]{1,0:T(8,128)(2,1)S(1)}, bf16[4096,256]{1,0:T(8,128)(2,1)}, u32[]{:S(2)}) copy-start(bf16[4096,256]{1,0:T(8,128)(2,1)} %all-gather.2.cloned.1.call-done) | copy-start | bytes 6291460
Sparse Core Ops, SparseCore 0:
  21.7 23.0 reduce-scatter.1
  51.0 41.4 all-gather.1
where the time goes:
time: 111 us
  waiting for transfers between devices  64.9 us (58%)
  local copies, waits for them, and re-layouts  17.6 us (16%)
  between operations  13.5 us (12%)
  other arithmetic  8.16 us (7%)
  matrix products  6.46 us (6%)
    all_gather x1, waiting for transfers between devices, shards(): lax.all_gather(panel, 'chan', axis=0, tiled=True)  41.6 us
    reduce_scatter x1, waiting for transfers between devices, shards(): lax.psum_scatter(partial_sum.reshape(chans * windows, own_rows * lax.axis...  23.2 us
    reshape x1, local copies, waits for them, and re-layouts, shards(): flat = strain.reshape(chans * windows, samp_dev)  6.86 us
    broadcast_in_dim x1, local copies, waits for them, and re-layouts, shards(): return result[None]  6.31 us
    dot_general x1, matrix products, shards(): jnp.dot(flat, table.reshape(samp_dev, own_rows * lax.axis_size('band') *...  3.73 us
    dot_general x1, matrix products, cross_block(): jnp.einsum('gb,ozb->ogz', local_panel_rows, stacked_spectra, preferred_el...  2.73 us
    another operation x1, other arithmetic  2.25 us
  transfers between devices with their start and end apart: 2, of which 2 were waited for; matrix products, arithmetic and copies ran while one was open for 0% of the time, Pallas kernels for 0%

commit v1 on v0

v1 whole, which is shorter than its diff:
```python
import functools
import math

import jax
import jax.numpy as jnp
from jax import lax
from jax.experimental import pallas as pl
from jax.experimental.pallas import tpu as pltpu
from jax.sharding import PartitionSpec as P

WINDOW_SAMPLES = 4096
K = 32
CHUNKS = 4
MESH = pl.DeviceIdType.MESH


def cos_turns(m):
    half, quarter = WINDOW_SAMPLES // 2, WINDOW_SAMPLES // 4
    t = (jnp.abs(m - half) - quarter).astype(jnp.float32) * (math.pi / half)
    z = t * t
    p = jnp.float32(1.0 / math.factorial(13))
    for order in (11, 9, 7, 5, 3, 1):
        sign = 1.0 if order % 4 == 1 else -1.0
        p = p * z + jnp.float32(sign / math.factorial(order))
    return p * t


def gather_kernel(
    n, nb, start_ref, x_hbm, g_ref, pq_ref,
    xbuf, tab, spec, own, xs, xr,
    in_sem, xs_sem, xr_sem, up_sem, down_sem, y_sem, core_sem, recv_sem,
):
    chans, windows, samp = xbuf.shape
    width = 2 * K
    cc = chans // CHUNKS
    cores = 2 if n % 2 == 0 else 1
    chips = n // cores
    inner = 2 if chips % 2 == 0 else 1
    outer = chips // inner
    me = lax.axis_index("chan")
    band = lax.axis_index("band")
    core = lax.rem(me, cores)
    chip = lax.div(me, cores)
    y = lax.rem(chip, inner)
    z = lax.div(chip, inner)

    def index(zz, yy, kk):
        return (zz * inner + yy) * cores + kk

    def load(k):
        rows = pl.ds(k * cc, cc)
        return pltpu.make_async_copy(x_hbm.at[rows], xbuf.at[rows], in_sem.at[k])

    for k in range(CHUNKS):
        load(k).start()

    barrier = pltpu.get_barrier_semaphore()
    up, down = index(z + 1, y, core), index(z - 1, y, core)
    y_peer, core_peer = index(z, inner - 1 - y, core), index(z, y, cores - 1 - core)
    has_up, has_down = z < outer - 1, z > 0
    for g in range(nb - 1):
        pl.semaphore_signal(
            barrier, inc=1, device_id={"band": lax.rem(band + 1 + g, nb)}, device_id_type=MESH
        )

    @pl.when(has_up)
    def _():
        pl.semaphore_signal(barrier, inc=1, device_id={"chan": up}, device_id_type=MESH)

    @pl.when(has_down)
    def _():
        pl.semaphore_signal(barrier, inc=1, device_id={"chan": down}, device_id_type=MESH)

    if inner > 1:
        pl.semaphore_signal(barrier, inc=1, device_id={"chan": y_peer}, device_id_type=MESH)
    if cores > 1:
        pl.semaphore_signal(barrier, inc=1, device_id={"chan": core_peer}, device_id_type=MESH)

    lane = lax.broadcasted_iota(jnp.int32, (1, nb * width), 1)
    freq = lane % K
    for g in range(nb):
        freq = freq + jnp.where(lane // width == g, start_ref[lax.rem(band + 1 + g, nb)], 0)
    shift = jnp.where((lane // K) % 2 == 1, WINDOW_SAMPLES // 4, 0)
    rows_at_once = min(256, samp)

    def fill(r, carry):
        base = pl.multiple_of(r * rows_at_once, rows_at_once)
        pos = band * samp + base + lax.broadcasted_iota(jnp.int32, (rows_at_once, nb * width), 0)
        taper = 0.5 - 0.5 * cos_turns(pos)
        m = (pos * freq + shift) & (WINDOW_SAMPLES - 1)
        tab[pl.ds(base, rows_at_once), :] = (taper * cos_turns(m)).astype(jnp.bfloat16)
        return carry

    lax.fori_loop(0, samp // rows_at_once, fill, 0)

    def band_copy(g, k):
        return pltpu.make_async_remote_copy(
            src_ref=xs.at[g, pl.ds(k * cc, cc)],
            dst_ref=xr.at[g, pl.ds(k * cc, cc)],
            send_sem=xs_sem.at[g, k],
            recv_sem=xr_sem.at[g, k],
            device_id={"band": lax.rem(band + 1 + g, nb)},
            device_id_type=MESH,
        )

    def send(src, k, sem, target):
        slot = g_ref.at[src, pl.ds(k * cc, cc)]
        return pltpu.make_async_remote_copy(
            src_ref=slot, dst_ref=slot, send_sem=sem, recv_sem=recv_sem.at[src, k],
            device_id={"chan": target}, device_id_type=MESH,
        )

    def send_up(d, k):
        return send(index(z - d, y, core), k, up_sem.at[d, k], up)

    def send_down(d, k):
        return send(index(z + d, y, core), k, down_sem.at[d, k], down)

    def send_y(d, k):
        return send(index(z + d, y, core), k, y_sem.at[d + outer - 1, k], y_peer)

    def send_core(far, d, k):
        yy = inner - 1 - y if far else y
        return send(index(z + d, yy, core), k, core_sem.at[far, d + outer - 1, k], core_peer)

    def in_line(d):
        return jnp.logical_and(z + d >= 0, z + d < outer)

    def arrived(zz, yy, kk, k):
        src = index(zz, yy, kk)
        send(src, k, y_sem.at[0, 0], y_peer if inner > 1 else core_peer).wait_recv()

    for k in range(CHUNKS):
        load(k).wait()
        x = xbuf[pl.ds(k * cc, cc)].reshape(cc * windows, samp)
        sums = jnp.dot(x, tab[...], preferred_element_type=jnp.float32)
        tiles, _, lanes = spec.shape
        for t in range(tiles):
            spec[t] = sums[:, t * lanes : (t + 1) * lanes]
        per_tile = lanes // width
        for g in range(nb):
            t, at = g // per_tile, g % per_tile * width
            parts = [spec[t, pl.ds(w, cc, stride=windows), :] for w in range(windows)]
            packed = jnp.concatenate([p[:, at : at + width] for p in parts], axis=1)
            if g < nb - 1:
                xs[g, pl.ds(k * cc, cc), :] = packed
            else:
                own[pl.ds(k * cc, cc), :] = packed
        if k == 0:
            pl.semaphore_wait(
                barrier,
                nb - 1 + (inner - 1) + (cores - 1) + has_up.astype(jnp.int32) + has_down.astype(jnp.int32),
            )
        for g in range(nb - 1):
            band_copy(g, k).start()

    def own_chunk(k):
        rows = pl.ds(k * cc, cc)
        total = own[rows, :]
        for g in range(nb - 1):
            band_copy(g, k).wait_recv()
            total = total + xr[g, rows, :]
        white = []
        for w in range(windows):
            s = total[:, w * width : (w + 1) * width]
            power = jnp.sum(s * s, axis=1, keepdims=True) * (1.0 / width)
            white.append(s * lax.rsqrt(power + 1e-06))
        panel = jnp.concatenate(white, axis=1)
        g_ref[me, rows, :] = panel.astype(jnp.bfloat16)

        @pl.when(has_up)
        def _():
            send_up(0, k).start()

        @pl.when(has_down)
        def _():
            send_down(0, k).start()

        if inner > 1:
            send_y(0, k).start()
        if cores > 1:
            send_core(0, 0, k).start()
        feats = panel.shape[1]
        is_real = lax.broadcasted_iota(jnp.int32, panel.shape, 1) % width < K
        rotated = jnp.where(
            is_real, pltpu.roll(panel, feats - K, axis=1), -pltpu.roll(panel, K, axis=1)
        )
        pq_ref[0, rows, :] = panel.astype(jnp.bfloat16)
        pq_ref[1, rows, :] = rotated.astype(jnp.bfloat16)

    def line_chunk(d, k):
        @pl.when(in_line(d))
        def _():
            arrived(z + d, y, core, k)
            if d < 0:
                pl.when(has_up)(lambda: send_up(-d, k).start())
            else:
                pl.when(has_down)(lambda: send_down(d, k).start())
            if inner > 1:
                send_y(d, k).start()
            if cores > 1:
                send_core(0, d, k).start()

    def far_chunk(d, k):
        @pl.when(in_line(d))
        def _():
            arrived(z + d, inner - 1 - y, core, k)
            if cores > 1:
                send_core(1, d, k).start()

    events = []
    for k in range(CHUNKS):
        events.append((1.4 * k, 0, own_chunk, (k,)))
        for d in range(1, outer):
            for s in (-d, d):
                events.append((1.4 * k + 2.2 * d, 1, line_chunk, (s, k)))
        if inner > 1:
            for d in range(outer):
                for s in {-d, d}:
                    events.append((1.4 * k + 2.2 * d + 2.3, 2, far_chunk, (s, k)))
    for _, _, run, args in sorted(events, key=lambda e: (e[0], e[1], e[3])):
        run(*args)

    if cores > 1:
        for k in range(CHUNKS):
            for yy in range(inner):
                for zz in range(outer):
                    arrived(zz, yy, cores - 1 - core, k)

    for k in range(CHUNKS):
        for g in range(nb - 1):
            band_copy(g, k).wait_send()
        for d in range(outer):
            pl.when(jnp.logical_and(in_line(-d), has_up))(lambda: send_up(d, k).wait_send())
            pl.when(jnp.logical_and(in_line(d), has_down))(lambda: send_down(d, k).wait_send())
        for d in range(1 - outer, outer):
            @pl.when(in_line(d))
            def _():
                if inner > 1:
                    send_y(d, k).wait_send()
                if cores > 1:
                    for far in range(inner):
                        send_core(far, d, k).wait_send()


def gather_panels(n, nb, strain, band_start):
    chans, windows, samp = strain.shape
    width = 2 * K
    feats = windows * width
    outer = n
    for _ in range(2):
        outer = outer // 2 if outer % 2 == 0 else outer
    dma = pltpu.SemaphoreType.DMA
    return pl.pallas_call(
        functools.partial(gather_kernel, n, nb),
        out_shape=(
            jax.ShapeDtypeStruct((n, chans, feats), jnp.bfloat16),
            jax.ShapeDtypeStruct((2, chans, feats), jnp.bfloat16),
        ),
        in_specs=[
            pl.BlockSpec(memory_space=pltpu.SMEM),
            pl.BlockSpec(memory_space=pl.ANY),
        ],
        out_specs=(
            pl.BlockSpec(memory_space=pltpu.VMEM),
            pl.BlockSpec(memory_space=pltpu.VMEM),
        ),
        scratch_shapes=[
            pltpu.VMEM((chans, windows, samp), jnp.bfloat16),
            pltpu.VMEM((samp, nb * width), jnp.bfloat16),
            pltpu.VMEM((nb * width // 128, chans // CHUNKS * windows, 128), jnp.float32),
            pltpu.VMEM((chans, feats), jnp.float32),
            pltpu.VMEM((nb - 1, chans, feats), jnp.float32),
            pltpu.VMEM((nb - 1, chans, feats), jnp.float32),
            dma((CHUNKS,)),
            dma((nb - 1, CHUNKS)),
            dma((nb - 1, CHUNKS)),
            dma((outer, CHUNKS)),
            dma((outer, CHUNKS)),
            dma((2 * outer - 1, CHUNKS)),
            dma((2, 2 * outer - 1, CHUNKS)),
            dma((n, CHUNKS)),
        ],
        compiler_params=pltpu.CompilerParams(
            collective_id=0, has_side_effects=True, vmem_limit_bytes=48 << 20
        ),
    )(band_start, strain)


def gram_kernel(pq_ref, g_ref, o_ref):
    two, chans, feats = pq_ref.shape
    product = lax.dot_general(
        pq_ref[...].reshape(two * chans, feats),
        g_ref[...],
        (((1,), (1,)), ((), ())),
        preferred_element_type=jnp.float32,
    )
    o_ref[...] = (product * (1.0 / (2.0 * K))).astype(jnp.bfloat16).reshape(o_ref.shape)


def gram(pq, panels):
    two, chans, feats = pq.shape
    total = panels.shape[0]
    cols = min(512, total)
    return pl.pallas_call(
        gram_kernel,
        out_shape=jax.ShapeDtypeStruct((1, two, chans, total), jnp.bfloat16),
        grid=(total // cols,),
        in_specs=[
            pl.BlockSpec((two, chans, feats), lambda i: (0, 0, 0)),
            pl.BlockSpec((cols, feats), lambda i: (i, 0)),
        ],
        out_specs=pl.BlockSpec((1, two, chans, cols), lambda i: (0, 0, 0, i)),
    )(pq, panels)


def shards(n, nb, strain, band_start):
    panels, pq = gather_panels(n, nb, strain, band_start)
    return gram(pq, panels.reshape(-1, panels.shape[2]))


def solution(mesh):
    return jax.shard_map(
        functools.partial(shards, mesh.shape["chan"], mesh.shape["band"]),
        mesh=mesh,
        in_specs=(P("chan", None, "band"), P()),
        out_specs=P("band", None, "chan", None),
        check_vma=False,
    )
```

time: 111 us -> 40.4 us (0.36)
  waiting for transfers between devices: 64.9 us -> 0 us
  Pallas kernels: 0 us -> 37.4 us
  local copies, waits for them, and re-layouts: 17.6 us -> 2.7 us
  between operations: 13.5 us -> 0.02 us
  other arithmetic: 8.16 us -> 0 us
  matrix products: 6.46 us -> 0 us
    all_gather x1 -> x0, waiting for transfers between devices: 41.6 us -> none  [shards(): lax.all_gather(panel, 'chan', axis=0, tiled=True)]
    pallas_call x0 -> x2, Pallas kernels: none -> 37.4 us  [the longest x1 30.2 us: gather_panels(): pl.pallas_call(functools.partial(gather_kernel, n, nb), out_shape=(jax.Sh...]
    reduce_scatter x1 -> x0, waiting for transfers between devices: 23.2 us -> none  [shards(): lax.psum_scatter(partial_sum.reshape(chans * windows, own_rows * lax.axis...]
    reshape x3 -> x0, local copies, waits for them, and re-layouts: 8.94 us -> none  [the longest x1 6.86 us: shards(): flat = strain.reshape(chans * windows, samp_dev)]
    dot_general x2 -> x0, matrix products: 6.46 us -> none  [the longest x1 3.73 us: shards(): jnp.dot(flat, table.reshape(samp_dev, own_rows * lax.axis_size('band') *...]
    broadcast_in_dim x1 -> x0, local copies, waits for them, and re-layouts: 6.31 us -> none  [shards(): return result[None]]
    unnamed x2 -> x6, local copies, waits for them, and re-layouts: 0.09 us -> 2.7 us
    another operation x2 -> x0, other arithmetic: 2.48 us -> none
  transfers between devices with their start and end apart: 2 -> 0, of which waited for: 2 -> 0; matrix products, arithmetic and copies ran while one was open for 0% -> 0% of each run, Pallas kernels for 0% -> 0%
where the time goes in v1:
time: 40.4 us; the launch traced here: 40.2 us
  Pallas kernels  37.4 us (93%)
  local copies, waits for them, and re-layouts  2.7 us (7%)
    pallas_call x1, Pallas kernels, gather_panels(): pl.pallas_call(functools.partial(gather_kernel, n, nb), out_shape=(jax.Sh...  30.2 us
    pallas_call x1, Pallas kernels, gram(): pl.pallas_call(gram_kernel, out_shape=jax.ShapeDtypeStruct((1, two, chans...  7.22 us
    unnamed x6, local copies, waits for them, and re-layouts  2.7 us

profile of v1, /device:TPU:0, one launch (start us, length us, event | category | flops | bytes accessed | tf_op | source)
XLA Modules:
  0.0 40.2 jit_solution(12691426847911610848)
XLA Ops:
  0.0 0.0 copy-start.2
  0.0 0.7 %copy-done.2 = s32[2]{0:T(128)S(1)} copy-done((s32[2]{0:T(128)S(1)}, s32[2]{0:T(128)}, u32[]{:S(2)}) %copy-start.2) | copy-done | bytes 32
  0.7 30.2 %shard_map.28 = (bf16[16,256,256]{2,1,0:T(8,128)(2,1)S(1)}, bf16[2,256,256]{2,1,0:T(8,128)(2,1)S(1)}) custom-call(s32[2]{0:T(128)S(1)} %copy-done.2, bf16[256,4,2048]{2,1,0:T(4,128)(2,1)} %x_hbm.1), custom_call_target="tpu_custom_call" | custom-call | tf_op jit(solution)/shard_map/pallas_call | solution.py:254
  30.9 0.0 copy-start
  30.9 1.3 %copy-done = bf16[16,256,256]{2,1,0:T(8,128)(2,1)} copy-done((bf16[16,256,256]{2,1,0:T(8,128)(2,1)}, bf16[16,256,256]{2,1,0:T(8,128)(2,1)S(1)}, u32[]{:S(2)}) %copy-start) | copy-done | bytes 2097176
  32.2 0.0 copy-start.1
  32.2 0.7 %copy-done.1 = bf16[2,256,256]{2,1,0:T(8,128)(2,1)} copy-done((bf16[2,256,256]{2,1,0:T(8,128)(2,1)}, bf16[2,256,256]{2,1,0:T(8,128)(2,1)S(1)}, u32[]{:S(2)}) %copy-start.1) | copy-done | bytes 262168
  32.9 7.2 %shard_map.29 = bf16[1,2,256,4096]{3,2,1,0:T(8,128)(2,1)} custom-call(bf16[2,256,256]{2,1,0:T(8,128)(2,1)} %copy-done.1, bf16[4096,256]{1,0:T(8,128)(2,1)} %bitcast.1), custom_call_target="tpu_custom_call" | custom-call | tf_op jit(solution)/shard_map/pallas_call | solution.py:305
Async XLA Ops:
  0.0 0.7 %copy-start.2 = (s32[2]{0:T(128)S(1)}, s32[2]{0:T(128)}, u32[]{:S(2)}) copy-start(s32[2]{0:T(128)} %start_ref.1) | copy-start | bytes 28
  30.9 1.3 %copy-start = (bf16[16,256,256]{2,1,0:T(8,128)(2,1)}, bf16[16,256,256]{2,1,0:T(8,128)(2,1)S(1)}, u32[]{:S(2)}) copy-start(bf16[16,256,256]{2,1,0:T(8,128)(2,1)S(1)} %get-tuple-element.8) | copy-start | bytes 6291460
  32.2 0.7 %copy-start.1 = (bf16[2,256,256]{2,1,0:T(8,128)(2,1)}, bf16[2,256,256]{2,1,0:T(8,128)(2,1)S(1)}, u32[]{:S(2)}) copy-start(bf16[2,256,256]{2,1,0:T(8,128)(2,1)S(1)} %get-tuple-element.7.pq_ref) | copy-start | bytes 786436

commit v2 on v1

--- a/solution.py
+++ b/solution.py
@@ -11,6 +11,7 @@
 WINDOW_SAMPLES = 4096
 K = 32
 CHUNKS = 4
+PAIR = 2
 MESH = pl.DeviceIdType.MESH
 
 
@@ -26,8 +27,8 @@
 
 
 def gather_kernel(
-    n, nb, start_ref, x_hbm, g_ref, pq_ref,
-    xbuf, tab, spec, own, xs, xr,
+    n, nb, start_ref, x_hbm, o_ref,
+    xbuf, trig, bases, tab, spec, own, xs, xr, g_ref, pq_ref,
     in_sem, xs_sem, xr_sem, up_sem, down_sem, y_sem, core_sem, recv_sem,
 ):
     chans, windows, samp = xbuf.shape
@@ -81,17 +82,30 @@
     for g in range(nb):
         freq = freq + jnp.where(lane // width == g, start_ref[lax.rem(band + 1 + g, nb)], 0)
     shift = jnp.where((lane // K) % 2 == 1, WINDOW_SAMPLES // 4, 0)
-    rows_at_once = min(256, samp)
+    step = trig.shape[1]
+    steps = samp // step
+    offset = lax.broadcasted_iota(jnp.int32, (step, nb * width), 0)
+    base = band * samp + step * lax.broadcasted_iota(jnp.int32, (steps, nb * width), 0)
+    wrap, lag = WINDOW_SAMPLES - 1, 3 * (WINDOW_SAMPLES // 4)
+    angle = offset * freq + shift
+    trig[0] = cos_turns(angle & wrap)
+    trig[1] = cos_turns((angle + lag) & wrap)
+    trig[2] = 0.5 * cos_turns(offset & wrap)
+    trig[3] = 0.5 * cos_turns((offset + lag) & wrap)
+    angle = base * freq
+    bases[0] = cos_turns(angle & wrap)
+    bases[1] = cos_turns((angle + lag) & wrap)
+    bases[2] = cos_turns(base & wrap)
+    bases[3] = cos_turns((base + lag) & wrap)
 
     def fill(r, carry):
-        base = pl.multiple_of(r * rows_at_once, rows_at_once)
-        pos = band * samp + base + lax.broadcasted_iota(jnp.int32, (rows_at_once, nb * width), 0)
-        taper = 0.5 - 0.5 * cos_turns(pos)
-        m = (pos * freq + shift) & (WINDOW_SAMPLES - 1)
-        tab[pl.ds(base, rows_at_once), :] = (taper * cos_turns(m)).astype(jnp.bfloat16)
+        turn = [bases[i, pl.ds(r, 1), :] for i in range(4)]
+        taper = 0.5 - (trig[2] * turn[2] - trig[3] * turn[3])
+        wave = trig[0] * turn[0] - trig[1] * turn[1]
+        tab[pl.ds(pl.multiple_of(r * step, step), step), :] = (taper * wave).astype(jnp.bfloat16)
         return carry
 
-    lax.fori_loop(0, samp // rows_at_once, fill, 0)
+    lax.fori_loop(0, steps, fill, 0, unroll=2)
 
     def band_copy(g, k):
         return pltpu.make_async_remote_copy(
@@ -208,24 +222,76 @@
             if cores > 1:
                 send_core(1, d, k).start()
 
-    events = []
+    def gram(src, h):
+        cols = PAIR * cc
+        two, _, feats = pq_ref.shape
+        product = lax.dot_general(
+            pq_ref[...].reshape(two * chans, feats),
+            g_ref[src, pl.ds(h * cols, cols), :],
+            (((1,), (1,)), ((), ())),
+            preferred_element_type=jnp.float32,
+        )
+        product = (product * (1.0 / width)).astype(jnp.bfloat16)
+        at = pl.ds(pl.multiple_of(src * chans + h * cols, cols), cols)
+        for i in range(two):
+            o_ref[i, :, at] = product[i * chans : (i + 1) * chans]
+
+    def near_gram(d, h):
+        pl.when(in_line(d))(lambda: gram(index(z + d, y, core), h))
+
+    def far_gram(d, h):
+        pl.when(in_line(d))(lambda: gram(index(z + d, inner - 1 - y, core), h))
+
+    def peer_gram(far, d, h):
+        @pl.when(in_line(d))
+        def _():
+            yy = inner - 1 - y if far else y
+            for k in range(PAIR * h, PAIR * h + PAIR):
+                arrived(z + d, yy, cores - 1 - core, k)
+            gram(index(z + d, yy, cores - 1 - core), h)
+
+    hop, wire, gap, cost = 1.6, 0.7, 1.4, 0.3
+    moves, jobs = [], []
+    near, far = {}, {}
     for k in range(CHUNKS):
-        events.append((1.4 * k, 0, own_chunk, (k,)))
-        for d in range(1, outer):
-            for s in (-d, d):
-                events.append((1.4 * k + 2.2 * d, 1, line_chunk, (s, k)))
-        if inner > 1:
-            for d in range(outer):
-                for s in {-d, d}:
-                    events.append((1.4 * k + 2.2 * d + 2.3, 2, far_chunk, (s, k)))
-    for _, _, run, args in sorted(events, key=lambda e: (e[0], e[1], e[3])):
+        for d in range(outer):
+            near[d, k] = gap * k + (hop + wire) * d
+    free = 0.0
+    for d, k in sorted(near, key=lambda e: (near[e], e)):
+        free = max(free, near[d, k]) + wire
+        far[d, k] = free + hop
+    for (d, k), t in near.items():
+        if d == 0:
+            moves.append((t, 0, own_chunk, (k,)))
+        else:
+            moves += [(t, 1, line_chunk, (s, k)) for s in (-d, d)]
+    if inner > 1:
+        for (d, k), t in far.items():
+            moves += [(t, 2, far_chunk, (s, k)) for s in sorted({-d, d})]
+    ready = near[0, CHUNKS - 1]
+    for h in range(CHUNKS // PAIR):
+        last = PAIR * h + PAIR - 1
+        for d in range(outer):
+            for s in sorted({-d, d}):
+                jobs.append((max(ready, near[d, last]), 0, near_gram, (s, h)))
+                if inner > 1:
+                    jobs.append((max(ready, far[d, last]), 1, far_gram, (s, h)))
+                if cores > 1:
+                    for f, times in enumerate((near, far)[:inner]):
+                        jobs.append((max(ready, times[d, last] + hop), 2, peer_gram, (f, s, h)))
+    order = lambda e: (e[0], e[1], e[3])
+    moves.sort(key=order)
+    jobs.sort(key=order)
+    now = 0.0
+    for t, _, run, args in moves:
+        while jobs and jobs[0][0] <= now and now + cost <= t:
+            _, _, job, what = jobs.pop(0)
+            job(*what)
+            now += cost / 2
         run(*args)
-
-    if cores > 1:
-        for k in range(CHUNKS):
-            for yy in range(inner):
-                for zz in range(outer):
-                    arrived(zz, yy, cores - 1 - core, k)
+        now = max(now, t)
+    for _, _, job, what in jobs:
+        job(*what)
 
     for k in range(CHUNKS):
         for g in range(nb - 1):
@@ -243,7 +309,7 @@
                         send_core(far, d, k).wait_send()
 
 
-def gather_panels(n, nb, strain, band_start):
+def cross_spectra(n, nb, strain, band_start):
     chans, windows, samp = strain.shape
     width = 2 * K
     feats = windows * width
@@ -253,25 +319,23 @@
     dma = pltpu.SemaphoreType.DMA
     return pl.pallas_call(
         functools.partial(gather_kernel, n, nb),
-        out_shape=(
-            jax.ShapeDtypeStruct((n, chans, feats), jnp.bfloat16),
-            jax.ShapeDtypeStruct((2, chans, feats), jnp.bfloat16),
-        ),
+        out_shape=jax.ShapeDtypeStruct((2, chans, n * chans), jnp.bfloat16),
         in_specs=[
             pl.BlockSpec(memory_space=pltpu.SMEM),
             pl.BlockSpec(memory_space=pl.ANY),
         ],
-        out_specs=(
-            pl.BlockSpec(memory_space=pltpu.VMEM),
-            pl.BlockSpec(memory_space=pltpu.VMEM),
-        ),
+        out_specs=pl.BlockSpec(memory_space=pltpu.VMEM),
         scratch_shapes=[
             pltpu.VMEM((chans, windows, samp), jnp.bfloat16),
+            pltpu.VMEM((4, min(64, samp), nb * width), jnp.float32),
+            pltpu.VMEM((4, samp // min(64, samp), nb * width), jnp.float32),
             pltpu.VMEM((samp, nb * width), jnp.bfloat16),
             pltpu.VMEM((nb * width // 128, chans // CHUNKS * windows, 128), jnp.float32),
             pltpu.VMEM((chans, feats), jnp.float32),
             pltpu.VMEM((nb - 1, chans, feats), jnp.float32),
             pltpu.VMEM((nb - 1, chans, feats), jnp.float32),
+            pltpu.VMEM((n, chans, feats), jnp.bfloat16),
+            pltpu.VMEM((2, chans, feats), jnp.bfloat16),
             dma((CHUNKS,)),
             dma((nb - 1, CHUNKS)),
             dma((nb - 1, CHUNKS)),
@@ -287,36 +351,34 @@
     )(band_start, strain)
 
 
-def gram_kernel(pq_ref, g_ref, o_ref):
-    two, chans, feats = pq_ref.shape
-    product = lax.dot_general(
-        pq_ref[...].reshape(two * chans, feats),
-        g_ref[...],
-        (((1,), (1,)), ((), ())),
-        preferred_element_type=jnp.float32,
-    )
-    o_ref[...] = (product * (1.0 / (2.0 * K))).astype(jnp.bfloat16).reshape(o_ref.shape)
-
-
-def gram(pq, panels):
-    two, chans, feats = pq.shape
-    total = panels.shape[0]
-    cols = min(512, total)
+def write_kernel(pieces, held, out, sem):
+    two, chans, _ = held.shape
+    rows = chans // pieces
+    copies = []
+    for i in range(two):
+        for p in range(pieces):
+            at = pl.ds(p * rows, rows)
+            copies.append(pltpu.make_async_copy(held.at[i, at], out.at[0, i, at], sem.at[i, p]))
+    for copy in copies:
+        copy.start()
+    for copy in copies:
+        copy.wait()
+
+
+def write_out(held):
+    pieces = 8
     return pl.pallas_call(
-        gram_kernel,
-        out_shape=jax.ShapeDtypeStruct((1, two, chans, total), jnp.bfloat16),
-        grid=(total // cols,),
-        in_specs=[
-            pl.BlockSpec((two, chans, feats), lambda i: (0, 0, 0)),
-            pl.BlockSpec((cols, feats), lambda i: (i, 0)),
-        ],
-        out_specs=pl.BlockSpec((1, two, chans, cols), lambda i: (0, 0, 0, i)),
-    )(pq, panels)
+        functools.partial(write_kernel, pieces),
+        out_shape=jax.ShapeDtypeStruct((1,) + held.shape, held.dtype),
+        in_specs=[pl.BlockSpec(memory_space=pl.ANY)],
+        out_specs=pl.BlockSpec(memory_space=pl.ANY),
+        scratch_shapes=[pltpu.SemaphoreType.DMA((held.shape[0], pieces))],
+        compiler_params=pltpu.CompilerParams(vmem_limit_bytes=1 << 20),
+    )(held)
 
 
 def shards(n, nb, strain, band_start):
-    panels, pq = gather_panels(n, nb, strain, band_start)
-    return gram(pq, panels.reshape(-1, panels.shape[2]))
+    return write_out(cross_spectra(n, nb, strain, band_start))
 
 
 def solution(mesh):

time: 40.4 us -> 34.8 us (0.86)
  Pallas kernels: 37.4 us -> 34 us
  local copies, waits for them, and re-layouts: 2.7 us -> 0.65 us
    pallas_call x2, Pallas kernels: 37.4 us -> 34 us  [the longest x1 31.9 us: cross_spectra(): pl.pallas_call(functools.partial(gather_kernel, n, nb), out_shape=jax.Sha...]
    unnamed x6 -> x2, local copies, waits for them, and re-layouts: 2.7 us -> 0.65 us
where the time goes in v2:
time: 34.8 us; the launch traced here: 34.7 us
  Pallas kernels  34 us (98%)
  local copies, waits for them, and re-layouts  0.65 us (2%)
    pallas_call x1, Pallas kernels, cross_spectra(): pl.pallas_call(functools.partial(gather_kernel, n, nb), out_shape=jax.Sha...  31.9 us
    pallas_call x1, Pallas kernels, write_out(): pl.pallas_call(functools.partial(write_kernel, pieces), out_shape=jax.Sha...  2.14 us

profile of v2, /device:TPU:0, one launch (start us, length us, event | category | flops | bytes accessed | tf_op | source)
XLA Modules:
  0.0 34.7 jit_solution(5594274074480722975)
XLA Ops:
  0.0 0.0 copy-start
  0.0 0.7 %copy-done = s32[2]{0:T(128)S(1)} copy-done((s32[2]{0:T(128)S(1)}, s32[2]{0:T(128)}, u32[]{:S(2)}) %copy-start) | copy-done | bytes 32
  0.7 31.9 %shard_map.28.held = bf16[2,256,4096]{2,1,0:T(8,128)(2,1)S(1)} custom-call(s32[2]{0:T(128)S(1)} %copy-done, bf16[256,4,2048]{2,1,0:T(4,128)(2,1)} %x_hbm.1), custom_call_target="tpu_custom_call" | custom-call | tf_op jit(solution)/shard_map/pallas_call | solution.py:320
  32.5 2.1 %shard_map.29 = bf16[1,2,256,4096]{3,2,1,0:T(8,128)(2,1)} custom-call(bf16[2,256,4096]{2,1,0:T(8,128)(2,1)S(1)} %shard_map.28.held), custom_call_target="tpu_custom_call" | custom-call | tf_op jit(solution)/shard_map/pallas_call | solution.py:370
Async XLA Ops:
  0.0 0.7 %copy-start = (s32[2]{0:T(128)S(1)}, s32[2]{0:T(128)}, u32[]{:S(2)}) copy-start(s32[2]{0:T(128)} %start_ref.1) | copy-start | bytes 28

commit v3 on v2

--- a/solution.py
+++ b/solution.py
@@ -10,8 +10,10 @@
 
 WINDOW_SAMPLES = 4096
 K = 32
-CHUNKS = 4
-PAIR = 2
+EIGHTHS = (1, 1, 2, 2, 2)
+CHUNKS = len(EIGHTHS)
+GROUPS = ((0, 1, 2), (3, 4))
+DETOUR = (2, 4)
 MESH = pl.DeviceIdType.MESH
 
 
@@ -27,13 +29,18 @@
 
 
 def gather_kernel(
-    n, nb, start_ref, x_hbm, o_ref,
+    n, nb, start_hbm, x_hbm, o_ref,
     xbuf, trig, bases, tab, spec, own, xs, xr, g_ref, pq_ref,
-    in_sem, xs_sem, xr_sem, up_sem, down_sem, y_sem, core_sem, recv_sem,
+    start_ref, start_sem, in_sem, xs_sem, xr_sem, up_sem, down_sem, y_sem, core_sem, detour_sem, recv_sem,
 ):
     chans, windows, samp = xbuf.shape
     width = 2 * K
-    cc = chans // CHUNKS
+    sizes = [chans * e // 8 for e in EIGHTHS]
+    starts = [sum(sizes[:k]) for k in range(CHUNKS)]
+
+    def rows_of(k):
+        return pl.ds(starts[k], sizes[k])
+
     cores = 2 if n % 2 == 0 else 1
     chips = n // cores
     inner = 2 if chips % 2 == 0 else 1
@@ -48,12 +55,17 @@
     def index(zz, yy, kk):
         return (zz * inner + yy) * cores + kk
 
+    detour = inner > 1 and outer % 2 == 0
+    buddy = z + 1 - 2 * lax.rem(z, 2)
+
     def load(k):
-        rows = pl.ds(k * cc, cc)
+        rows = rows_of(k)
         return pltpu.make_async_copy(x_hbm.at[rows], xbuf.at[rows], in_sem.at[k])
 
     for k in range(CHUNKS):
         load(k).start()
+    first_bins = pltpu.make_async_copy(start_hbm, start_ref, start_sem)
+    first_bins.start()
 
     barrier = pltpu.get_barrier_semaphore()
     up, down = index(z + 1, y, core), index(z - 1, y, core)
@@ -77,6 +89,7 @@
     if cores > 1:
         pl.semaphore_signal(barrier, inc=1, device_id={"chan": core_peer}, device_id_type=MESH)
 
+    first_bins.wait()
     lane = lax.broadcasted_iota(jnp.int32, (1, nb * width), 1)
     freq = lane % K
     for g in range(nb):
@@ -109,8 +122,8 @@
 
     def band_copy(g, k):
         return pltpu.make_async_remote_copy(
-            src_ref=xs.at[g, pl.ds(k * cc, cc)],
-            dst_ref=xr.at[g, pl.ds(k * cc, cc)],
+            src_ref=xs.at[g, rows_of(k)],
+            dst_ref=xr.at[g, rows_of(k)],
             send_sem=xs_sem.at[g, k],
             recv_sem=xr_sem.at[g, k],
             device_id={"band": lax.rem(band + 1 + g, nb)},
@@ -118,7 +131,7 @@
         )
 
     def send(src, k, sem, target):
-        slot = g_ref.at[src, pl.ds(k * cc, cc)]
+        slot = g_ref.at[src, rows_of(k)]
         return pltpu.make_async_remote_copy(
             src_ref=slot, dst_ref=slot, send_sem=sem, recv_sem=recv_sem.at[src, k],
             device_id={"chan": target}, device_id_type=MESH,
@@ -137,6 +150,10 @@
         yy = inner - 1 - y if far else y
         return send(index(z + d, yy, core), k, core_sem.at[far, d + outer - 1, k], core_peer)
 
+    def send_detour(k):
+        src = index(z, inner - 1 - y, core)
+        return send(src, k, detour_sem.at[k], index(buddy, y, core))
+
     def in_line(d):
         return jnp.logical_and(z + d >= 0, z + d < outer)
 
@@ -146,20 +163,20 @@
 
     for k in range(CHUNKS):
         load(k).wait()
-        x = xbuf[pl.ds(k * cc, cc)].reshape(cc * windows, samp)
+        x = xbuf[rows_of(k)].reshape(sizes[k] * windows, samp)
         sums = jnp.dot(x, tab[...], preferred_element_type=jnp.float32)
         tiles, _, lanes = spec.shape
         for t in range(tiles):
-            spec[t] = sums[:, t * lanes : (t + 1) * lanes]
+            spec[t, pl.ds(0, sizes[k] * windows), :] = sums[:, t * lanes : (t + 1) * lanes]
         per_tile = lanes // width
         for g in range(nb):
             t, at = g // per_tile, g % per_tile * width
-            parts = [spec[t, pl.ds(w, cc, stride=windows), :] for w in range(windows)]
+            parts = [spec[t, pl.ds(w, sizes[k], stride=windows), :] for w in range(windows)]
             packed = jnp.concatenate([p[:, at : at + width] for p in parts], axis=1)
             if g < nb - 1:
-                xs[g, pl.ds(k * cc, cc), :] = packed
+                xs[g, rows_of(k), :] = packed
             else:
-                own[pl.ds(k * cc, cc), :] = packed
+                own[rows_of(k), :] = packed
         if k == 0:
             pl.semaphore_wait(
                 barrier,
@@ -169,7 +186,7 @@
             band_copy(g, k).start()
 
     def own_chunk(k):
-        rows = pl.ds(k * cc, cc)
+        rows = rows_of(k)
         total = own[rows, :]
         for g in range(nb - 1):
             band_copy(g, k).wait_recv()
@@ -211,7 +228,10 @@
             else:
                 pl.when(has_down)(lambda: send_down(d, k).start())
             if inner > 1:
-                send_y(d, k).start()
+                if detour and k in DETOUR:
+                    pl.when(z + d != buddy)(lambda: send_y(d, k).start())
+                else:
+                    send_y(d, k).start()
             if cores > 1:
                 send_core(0, d, k).start()
 
@@ -219,20 +239,22 @@
         @pl.when(in_line(d))
         def _():
             arrived(z + d, inner - 1 - y, core, k)
+            if d == 0 and detour and k in DETOUR:
+                send_detour(k).start()
             if cores > 1:
                 send_core(1, d, k).start()
 
     def gram(src, h):
-        cols = PAIR * cc
+        first, cols = starts[GROUPS[h][0]], sum(sizes[k] for k in GROUPS[h])
         two, _, feats = pq_ref.shape
         product = lax.dot_general(
             pq_ref[...].reshape(two * chans, feats),
-            g_ref[src, pl.ds(h * cols, cols), :],
+            g_ref[src, pl.ds(first, cols), :],
             (((1,), (1,)), ((), ())),
             preferred_element_type=jnp.float32,
         )
         product = (product * (1.0 / width)).astype(jnp.bfloat16)
-        at = pl.ds(pl.multiple_of(src * chans + h * cols, cols), cols)
+        at = pl.ds(pl.multiple_of(src * chans + first, cols), cols)
         for i in range(two):
             o_ref[i, :, at] = product[i * chans : (i + 1) * chans]
 
@@ -246,19 +268,20 @@
         @pl.when(in_line(d))
         def _():
             yy = inner - 1 - y if far else y
-            for k in range(PAIR * h, PAIR * h + PAIR):
+            for k in GROUPS[h]:
                 arrived(z + d, yy, cores - 1 - core, k)
             gram(index(z + d, yy, cores - 1 - core), h)
 
-    hop, wire, gap, cost = 1.6, 0.7, 1.4, 0.3
+    hop, cost = 1.6, 0.3
+    wire = [0.35 * e for e in EIGHTHS]
     moves, jobs = [], []
     near, far = {}, {}
     for k in range(CHUNKS):
         for d in range(outer):
-            near[d, k] = gap * k + (hop + wire) * d
+            near[d, k] = 2 * sum(wire[1 : k + 1]) + (hop + wire[k]) * d
     free = 0.0
     for d, k in sorted(near, key=lambda e: (near[e], e)):
-        free = max(free, near[d, k]) + wire
+        free = max(free, near[d, k]) + wire[k]
         far[d, k] = free + hop
     for (d, k), t in near.items():
         if d == 0:
@@ -269,8 +292,8 @@
         for (d, k), t in far.items():
             moves += [(t, 2, far_chunk, (s, k)) for s in sorted({-d, d})]
     ready = near[0, CHUNKS - 1]
-    for h in range(CHUNKS // PAIR):
-        last = PAIR * h + PAIR - 1
+    for h in range(len(GROUPS)):
+        last = GROUPS[h][-1]
         for d in range(outer):
             for s in sorted({-d, d}):
                 jobs.append((max(ready, near[d, last]), 0, near_gram, (s, h)))
@@ -303,7 +326,12 @@
             @pl.when(in_line(d))
             def _():
                 if inner > 1:
-                    send_y(d, k).wait_send()
+                    if detour and k in DETOUR:
+                        pl.when(z + d != buddy)(lambda: send_y(d, k).wait_send())
+                    else:
+                        send_y(d, k).wait_send()
+                if d == 0 and detour and k in DETOUR:
+                    send_detour(k).wait_send()
                 if cores > 1:
                     for far in range(inner):
                         send_core(far, d, k).wait_send()
@@ -321,7 +349,7 @@
         functools.partial(gather_kernel, n, nb),
         out_shape=jax.ShapeDtypeStruct((2, chans, n * chans), jnp.bfloat16),
         in_specs=[
-            pl.BlockSpec(memory_space=pltpu.SMEM),
+            pl.BlockSpec(memory_space=pl.ANY),
             pl.BlockSpec(memory_space=pl.ANY),
         ],
         out_specs=pl.BlockSpec(memory_space=pltpu.VMEM),
@@ -330,12 +358,14 @@
             pltpu.VMEM((4, min(64, samp), nb * width), jnp.float32),
             pltpu.VMEM((4, samp // min(64, samp), nb * width), jnp.float32),
             pltpu.VMEM((samp, nb * width), jnp.bfloat16),
-            pltpu.VMEM((nb * width // 128, chans // CHUNKS * windows, 128), jnp.float32),
+            pltpu.VMEM((nb * width // 128, chans * max(EIGHTHS) // 8 * windows, 128), jnp.float32),
             pltpu.VMEM((chans, feats), jnp.float32),
             pltpu.VMEM((nb - 1, chans, feats), jnp.float32),
             pltpu.VMEM((nb - 1, chans, feats), jnp.float32),
             pltpu.VMEM((n, chans, feats), jnp.bfloat16),
             pltpu.VMEM((2, chans, feats), jnp.bfloat16),
+            pltpu.SMEM(band_start.shape, jnp.int32),
+            dma,
             dma((CHUNKS,)),
             dma((nb - 1, CHUNKS)),
             dma((nb - 1, CHUNKS)),
@@ -343,6 +373,7 @@
             dma((outer, CHUNKS)),
             dma((2 * outer - 1, CHUNKS)),
             dma((2, 2 * outer - 1, CHUNKS)),
+            dma((CHUNKS,)),
             dma((n, CHUNKS)),
         ],
         compiler_params=pltpu.CompilerParams(

time: 34.8 us -> 36.1 us (1.037)
  Pallas kernels: 34 us -> 35.3 us
    pallas_call x1, Pallas kernels: 31.9 us -> 33.1 us  [cross_spectra(): pl.pallas_call(functools.partial(gather_kernel, n, nb), out_shape=jax.Sha...]
where the time goes in v3:
time: 36.1 us; the launch traced here: 35.9 us
  Pallas kernels  35.3 us (98%)
  local copies, waits for them, and re-layouts  0.65 us (2%)
    pallas_call x1, Pallas kernels, cross_spectra(): pl.pallas_call(functools.partial(gather_kernel, n, nb), out_shape=jax.Sha...  33.1 us
    pallas_call x1, Pallas kernels, write_out(): pl.pallas_call(functools.partial(write_kernel, pieces), out_shape=jax.Sha...  2.14 us

profile of v3, /device:TPU:0, one launch (start us, length us, event | category | flops | bytes accessed | tf_op | source)
XLA Modules:
  0.0 35.9 jit_solution(11625931575332348003)
XLA Ops:
  0.0 0.0 copy-start
  0.0 0.7 %copy-done = s32[2]{0:T(128)S(1)} copy-done((s32[2]{0:T(128)S(1)}, s32[2]{0:T(128)}, u32[]{:S(2)}) %copy-start) | copy-done | bytes 32
  0.7 33.1 %shard_map.28.held = bf16[2,256,4096]{2,1,0:T(8,128)(2,1)S(1)} custom-call(s32[2]{0:T(128)S(1)} %copy-done, bf16[256,4,2048]{2,1,0:T(4,128)(2,1)} %x_hbm.1), custom_call_target="tpu_custom_call" | custom-call | tf_op jit(solution)/shard_map/pallas_call | solution.py:348
  33.8 2.1 %shard_map.29 = bf16[1,2,256,4096]{3,2,1,0:T(8,128)(2,1)} custom-call(bf16[2,256,4096]{2,1,0:T(8,128)(2,1)S(1)} %shard_map.28.held), custom_call_target="tpu_custom_call" | custom-call | tf_op jit(solution)/shard_map/pallas_call | solution.py:401
Async XLA Ops:
  0.0 0.7 %copy-start = (s32[2]{0:T(128)S(1)}, s32[2]{0:T(128)}, u32[]{:S(2)}) copy-start(s32[2]{0:T(128)} %start_hbm.1) | copy-start | bytes 28

commit v4 on v3

--- a/solution.py
+++ b/solution.py
@@ -10,10 +10,10 @@
 
 WINDOW_SAMPLES = 4096
 K = 32
-EIGHTHS = (1, 1, 2, 2, 2)
+EIGHTHS = (2, 2, 2, 2)
 CHUNKS = len(EIGHTHS)
-GROUPS = ((0, 1, 2), (3, 4))
-DETOUR = (2, 4)
+GROUPS = ((0, 1, 2, 3),)
+DETOUR = (1, 3)
 MESH = pl.DeviceIdType.MESH
 
 

time: 36.1 us -> 31.7 us (0.88)
  Pallas kernels: 35.3 us -> 30.8 us
    pallas_call x1, Pallas kernels: 33.1 us -> 28.6 us  [cross_spectra(): pl.pallas_call(functools.partial(gather_kernel, n, nb), out_shape=jax.Sha...]
where the time goes in v4:
time: 31.7 us; the launch traced here: 31.4 us
  Pallas kernels  30.8 us (97%)
  local copies, waits for them, and re-layouts  0.65 us (2%)
    pallas_call x1, Pallas kernels, cross_spectra(): pl.pallas_call(functools.partial(gather_kernel, n, nb), out_shape=jax.Sha...  28.6 us
    pallas_call x1, Pallas kernels, write_out(): pl.pallas_call(functools.partial(write_kernel, pieces), out_shape=jax.Sha...  2.14 us
    unnamed x2, local copies, waits for them, and re-layouts  0.65 us

profile of v4, /device:TPU:0, one launch (start us, length us, event | category | flops | bytes accessed | tf_op | source)
XLA Modules:
  0.0 31.4 jit_solution(2313666964603621339)
XLA Ops:
  0.0 0.0 copy-start
  0.0 0.7 %copy-done = s32[2]{0:T(128)S(1)} copy-done((s32[2]{0:T(128)S(1)}, s32[2]{0:T(128)}, u32[]{:S(2)}) %copy-start) | copy-done | bytes 32
  0.7 28.6 %shard_map.28.held = bf16[2,256,4096]{2,1,0:T(8,128)(2,1)S(1)} custom-call(s32[2]{0:T(128)S(1)} %copy-done, bf16[256,4,2048]{2,1,0:T(4,128)(2,1)} %x_hbm.1), custom_call_target="tpu_custom_call" | custom-call | tf_op jit(solution)/shard_map/pallas_call | solution.py:348
  29.3 2.1 %shard_map.29 = bf16[1,2,256,4096]{3,2,1,0:T(8,128)(2,1)} custom-call(bf16[2,256,4096]{2,1,0:T(8,128)(2,1)S(1)} %shard_map.28.held), custom_call_target="tpu_custom_call" | custom-call | tf_op jit(solution)/shard_map/pallas_call | solution.py:401
Async XLA Ops:
  0.0 0.7 %copy-start = (s32[2]{0:T(128)S(1)}, s32[2]{0:T(128)}, u32[]{:S(2)}) copy-start(s32[2]{0:T(128)} %start_hbm.1) | copy-start | bytes 28
